TPU v7x, 32 devices: a whole 2x2x4 slice. The times are simulated.
32 devices in a mesh: span: 8 (over z, x), chord: 4 (over y, core).
Axes of the slice: x: 2, y: 2, z: 4, core: 2. Of those that a mesh axis runs over, the one named last changes fastest.
Arguments:
- pressure: float32 [2, 1024, 512], P(None, 'span', 'chord'), may hold values from 0 to 1
- fill_state: int32 [2, 1024, 512], P(None, 'span', 'chord'), may hold values from 0 to 2
- perm_class: int32 [2, 1024, 512], P(None, 'span', 'chord'), may hold values from 0 to 7
- perm_table: float32 [2, 8], replicated, may hold values from 1 to 4
- inlet_span: int32 [128], replicated, may hold values from 0 to 1023
- inlet_chord: int32 [128], replicated, may hold values from 0 to 511
- inlet_rate: float32 [128], replicated, may hold values from 500 to 1500
Outputs:
- pressure_out: float32 [2, 1024, 512], P(None, 'span', 'chord')
Inputs may be any that keep to these rules, and one draw needn't show every extreme that they name: `inlet_span`: inlet cells may repeat; their rates add.
All inputs are finite; a program needn't handle non-finite values.
Results may differ from a plain program's by a relative error of at most 0.00035.
Values sent between devices are 32-bit elements; how exact they have to be, the bound alone decides.
A program may use at most 64 MiB of HBM per device.

v0:
```python
import jax
import jax.numpy as jnp
from jax import lax
from jax.sharding import PartitionSpec as P

HALF_RATE = 200.0
COUPLE = 0.3


def shift_lower(values, stride):
    padding = jnp.zeros(values.shape[:-1] + (stride,), values.dtype)
    return jnp.concatenate([padding, values[..., :-stride]], axis=-1)


def shift_upper(values, stride):
    padding = jnp.zeros(values.shape[:-1] + (stride,), values.dtype)
    return jnp.concatenate([values[..., stride:], padding], axis=-1)


def faces(cond):
    summed = HALF_RATE * (cond + shift_upper(cond, 1))
    closing = jnp.zeros(cond.shape[:-1] + (1,), cond.dtype)
    return jnp.concatenate([summed[..., :-1], closing], axis=-1)


def parallel_cyclic_reduction_update(
    lower_band,
    diagonal_terms,
    upper_band,
    right_hand_side,
    previous_neighbour_row,
    next_neighbour_row,
):
    new_lower = -lower_band * previous_neighbour_row[0]
    new_diag = (
        diagonal_terms - lower_band * previous_neighbour_row[1] - upper_band * next_neighbour_row[0]
    )
    new_upper = -upper_band * next_neighbour_row[1]
    new_rhs = (
        right_hand_side
        - lower_band * previous_neighbour_row[2]
        - upper_band * next_neighbour_row[2]
    )
    return (new_lower, new_diag, new_upper, new_rhs)


def line_solve(lower_band, diagonal_terms, upper_band, right_hand_side):
    total = right_hand_side.shape[-1]
    stride = 1
    while stride < total:
        ratios = (
            lower_band / diagonal_terms,
            upper_band / diagonal_terms,
            right_hand_side / diagonal_terms,
        )
        previous_neighbour_row = [shift_lower(v, stride) for v in ratios]
        next_neighbour_row = [shift_upper(v, stride) for v in ratios]
        lower_band, diagonal_terms, upper_band, right_hand_side = parallel_cyclic_reduction_update(
            lower_band,
            diagonal_terms,
            upper_band,
            right_hand_side,
            previous_neighbour_row,
            next_neighbour_row,
        )
        stride = stride * 2
    return right_hand_side / diagonal_terms


def explicit_core(field, field_next, field_prev, faces_here, faces_prev, source):
    flux = faces_here * (field_next - field) - faces_prev * (field - field_prev)
    return field + flux + COUPLE * (jnp.flip(field, 0) - field) + source


def explicit_lines(field, faces_here, faces_prev, source):
    return explicit_core(
        field, shift_upper(field, 1), shift_lower(field, 1), faces_here, faces_prev, source
    )


def second_half(star, half_lines, source):
    return 2.0 * star - half_lines + COUPLE * (jnp.flip(star, 0) - star) + source


def to_span(block):
    turned = jnp.transpose(block, (0, 2, 1))
    return lax.all_to_all(turned, "span", split_axis=1, concat_axis=2, tiled=True)


def span_return(lines):
    turned = lax.all_to_all(lines, "span", split_axis=2, concat_axis=1, tiled=True)
    return jnp.transpose(turned, (0, 2, 1))


def to_chord(block):
    return lax.all_to_all(block, "chord", split_axis=1, concat_axis=2, tiled=True)


def from_chord(lines):
    return lax.all_to_all(lines, "chord", split_axis=2, concat_axis=1, tiled=True)


def per_device(pressure, fill_state, perm_class, perm_table, inlet_span, inlet_chord, inlet_rate):
    plies = pressure.shape[0]
    rows = pressure.shape[1]
    width = pressure.shape[2]
    mobility = jnp.where(fill_state == 0, 1.0, jnp.where(fill_state == 1, 0.5, 0.25))
    perm = jnp.zeros(pressure.shape, jnp.float32)
    for klass in range(perm_table.shape[1]):
        perm = perm + jnp.where(perm_class == klass, perm_table[:, klass][:, None, None], 0.0)
    cond = perm * mobility
    row_global = lax.axis_index("span") * rows + jnp.arange(rows, dtype=jnp.int32)
    col_global = lax.axis_index("chord") * width + jnp.arange(width, dtype=jnp.int32)
    row_hits = (row_global[:, None] == inlet_span[None, :]).astype(jnp.float32) * inlet_rate[
        None, :
    ]
    col_hits = (inlet_chord[:, None] == col_global[None, :]).astype(jnp.float32)
    plane = jnp.dot(
        row_hits, col_hits, precision=lax.Precision.HIGHEST, preferred_element_type=jnp.float32
    )
    source = plane[None]
    span_setup = to_span(jnp.concatenate([cond, source], axis=0))
    span_faces = faces(span_setup[:plies])
    span_prev = shift_lower(span_faces, 1)
    span_source = span_setup[plies:]
    span_diag = 1.0 + span_prev + span_faces
    chord_setup = to_chord(jnp.concatenate([cond, source, pressure], axis=0))
    chord_faces = faces(chord_setup[:plies])
    chord_prev = shift_lower(chord_faces, 1)
    chord_diag = 1.0 + chord_prev + chord_faces
    chord_source = chord_setup[plies : plies + 1]
    field = chord_setup[plies + 1 :]
    half = explicit_lines(field, chord_faces, chord_prev, chord_source)
    half_lines = to_span(from_chord(half))
    star = line_solve(-span_prev, span_diag, -span_faces, half_lines)
    second = second_half(star, half_lines, span_source)
    returned = to_chord(span_return(second))
    field = line_solve(-chord_prev, chord_diag, -chord_faces, returned)
    result = from_chord(field)
    return result


def solution(mesh):
    placed = (
        P(None, "span", "chord"),
        P(None, "span", "chord"),
        P(None, "span", "chord"),
        P(),
        P(),
        P(),
        P(),
    )
    return jax.shard_map(
        per_device, mesh=mesh, in_specs=placed, out_specs=P(None, "span", "chord"), check_vma=False
    )
```

profile of v0, /device:TPU:0, one launch (start us, length us, event | category | flops | bytes accessed | tf_op | source)
XLA Modules:
  0.0 96.3 jit_solution(14580648930356081755)
XLA Ops:
  0.0 0.7 copy-done.2
  0.7 0.3 slice_reduce_fusion.7
  1.0 1.0 %copy.86 = f32[2,128,128]{2,0,1:T(2,128)S(1)} copy(f32[2,128,128]{2,1,0:T(8,128)} %param.7) | data formatting | bytes 262144 | tf_op args[0]
  2.1 0.2 fusion.16
  2.4 0.6 copy-done
  3.0 0.6 fusion.13
  3.5 1.0 %pad_maximum_fusion = f32[5,128,128]{2,0,1:T(8,128)} fusion(f32[2,128,128]{2,0,1:T(2,128)S(1)} %copy.86, f32[1,128,128]{2,0,1:T(1,128)S(1)} %bitcast.122, f32[2,128,128]{2,0,1:T(2,128)S(1)} %fusion.13), kind=kLoop, calls=%fused_computation | loop fusion | flops 163840 | bytes 655360 | tf_op jit(solution)/shard_map/concatenate | solution.py:127
  4.5 4.3 %all-to-all-start = ((f32[5,128,128]{2,0,1:T(8,128)}), f32[5,128,128]{2,0,1:T(8,128)S(1)}, u32[]{:S(2)}, u32[]{:S(2)}) async-start(f32[5,128,128]{2,0,1:T(8,128)} %pad_maximum_fusion), calls=%async_computation | async-start | bytes 1048576 | tf_op jit(solution)/shard_map/all_to_all | solution.py:96
  8.9 0.9 copy.98
  9.8 7.8 %all-to-all-done = f32[5,128,128]{2,0,1:T(8,128)S(1)} async-done(((f32[5,128,128]{2,0,1:T(8,128)}), f32[5,128,128]{2,0,1:T(8,128)S(1)}, u32[]{:S(2)}, u32[]{:S(2)}) %all-to-all-start) | async-done | bytes 327712 | tf_op jit(solution)/shard_map/all_to_all | solution.py:96
  17.6 6.5 %all-to-all-start.3 = ((f32[3,128,128]{2,0,1:T(4,128)}), f32[3,128,128]{2,0,1:T(4,128)S(1)}, u32[]{:S(2)}, u32[]{:S(2)}) async-start(f32[3,128,128]{2,0,1:T(4,128)} %copy.98), calls=%async_computation.3 | async-start | bytes 524288 | tf_op jit(solution)/shard_map/all_to_all | solution.py:87
  24.5 0.6 copy-done.4
  25.2 0.1 fusion.2
  25.3 0.2 copy.91
  25.6 1.2 %reshape.34 = f32[4,1,8192]{2,1,0:T(1,128)} reshape(f32[512,2,32]{2,1,0:T(2,128)S(1)} %bitcast.97) | data formatting | bytes 262144
  26.8 5.9 %all-to-all-done.3 = f32[3,128,128]{2,0,1:T(4,128)S(1)} async-done(((f32[3,128,128]{2,0,1:T(4,128)}), f32[3,128,128]{2,0,1:T(4,128)S(1)}, u32[]{:S(2)}, u32[]{:S(2)}) %all-to-all-start.3) | async-done | bytes 196640 | tf_op jit(solution)/shard_map/all_to_all | solution.py:87
  32.7 3.3 %all-to-all-start.1 = ((f32[4,1,8192]{2,1,0:T(1,128)}), f32[4,1,8192]{2,1,0:T(1,128)S(1)}, u32[]{:S(2)}, u32[]{:S(2)}) async-start(f32[4,1,8192]{2,1,0:T(1,128)} %reshape.34), calls=%async_computation.1 | async-start | bytes 262144 | tf_op jit(solution)/shard_map/all_to_all | solution.py:100
  36.2 4.4 %all-to-all-done.1 = f32[4,1,8192]{2,1,0:T(1,128)S(1)} async-done(((f32[4,1,8192]{2,1,0:T(1,128)}), f32[4,1,8192]{2,1,0:T(1,128)S(1)}, u32[]{:S(2)}, u32[]{:S(2)}) %all-to-all-start.1) | async-done | bytes 131104 | tf_op jit(solution)/shard_map/all_to_all | solution.py:100
  40.6 0.6 broadcast.342
  41.2 1.0 %reduce.16 = f32[4,8192]{1,0:T(4,128)S(1)} reduce(f32[4,1,8192]{2,1,0:T(1,128)S(1)} %all-to-all-done.1, f32[]{:T(128)} %broadcast.342), dimensions={1}, to_apply=%all_to_all.90.reduce_sub_computation | reduce | bytes 262148 | tf_op jit(solution)/shard_map/all_to_all | solution.py:100
  42.2 0.5 reshape.35
  42.7 0.2 copy.111
  42.9 0.8 copy.94
  43.6 3.6 %all-to-all-start.2 = ((f32[2,128,128]{2,0,1:T(2,128)}), f32[2,128,128]{2,0,1:T(2,128)S(1)}, u32[]{:S(2)}, u32[]{:S(2)}) async-start(f32[2,128,128]{2,0,1:T(2,128)} %copy.94), calls=%async_computation.2 | async-start | bytes 262144 | tf_op jit(solution)/shard_map/all_to_all | solution.py:87
  47.2 7.3 %all-to-all-done.2 = f32[2,128,128]{2,0,1:T(2,128)S(1)} async-done(((f32[2,128,128]{2,0,1:T(2,128)}), f32[2,128,128]{2,0,1:T(2,128)S(1)}, u32[]{:S(2)}, u32[]{:S(2)}) %all-to-all-start.2) | async-done | bytes 131104 | tf_op jit(solution)/shard_map/all_to_all | solution.py:87
  54.6 0.7 copy-done.3
  55.7 0.2 fusion.44
  55.9 0.1 fusion.60
  56.3 0.1 fusion.43
  56.9 0.1 fusion.42
  58.0 0.1 fusion.40
  58.6 0.1 fusion.39
  59.2 0.1 fusion.38
  60.0 0.5 copy.102
  60.5 1.4 %reshape.36 = f32[8,1,4096]{2,1,0:T(1,128)S(1)} reshape(f32[1024,2,16]{2,1,0:T(2,128)S(1)} %bitcast.95) | data formatting | bytes 262144
  62.0 9.7 %all_to_all.120 = f32[8,1,4096]{2,1,0:T(1,128)S(1)} all-to-all(f32[8,1,4096]{2,1,0:T(1,128)S(1)} %reshape.36), channel_id=1, replica_groups=mesh['span'=8,'chord'=4] {'span'}, dimensions={0} | all-to-all | bytes 262144 | tf_op jit(solution)/shard_map/all_to_all | solution.py:91
  71.7 1.0 %reduce.17 = f32[8,4096]{1,0:T(8,128)S(1)} reduce(f32[8,1,4096]{2,1,0:T(1,128)S(1)} %all_to_all.120, f32[]{:T(128)} %broadcast.342), dimensions={1}, to_apply=%all_to_all.101.reduce_sub_computation | reduce | bytes 262148 | tf_op jit(solution)/shard_map/all_to_all | solution.py:91
  72.7 1.4 %reshape.37 = f32[1024,2,16]{2,1,0:T(2,128)S(1)} reshape(f32[8,4096]{1,0:T(8,128)S(1)} %reduce.17) | data formatting | bytes 262144
  74.1 0.4 copy.113
  74.6 7.0 %all_to_all.121 = f32[2,128,128]{2,0,1:T(2,128)S(1)} all-to-all(f32[2,128,128]{2,0,1:T(2,128)S(1)} %copy.105), channel_id=1, replica_groups=mesh['span'=8,'chord'=4] {'chord'}, dimensions={1} | all-to-all | bytes 262144 | tf_op jit(solution)/shard_map/all_to_all | solution.py:96
  82.1 0.2 fusion.34
  86.2 0.2 copy.108
  86.4 0.5 reshape.38
  87.0 7.0 %all_to_all.122 = f32[4,1,8192]{2,1,0:T(1,128)S(1)} all-to-all(f32[4,1,8192]{2,1,0:T(1,128)S(1)} %reshape.38), channel_id=1, replica_groups=mesh['span'=8,'chord'=4] {'chord'}, dimensions={0} | all-to-all | bytes 262144 | tf_op jit(solution)/shard_map/all_to_all | solution.py:100
  94.0 1.0 %reduce.18 = f32[4,8192]{1,0:T(4,128)S(1)} reduce(f32[4,1,8192]{2,1,0:T(1,128)S(1)} %all_to_all.122, f32[]{:T(128)} %broadcast.342), dimensions={1}, to_apply=%all_to_all.109.reduce_sub_computation | reduce | bytes 262148 | tf_op jit(solution)/shard_map/all_to_all | solution.py:100
  95.0 0.5 reshape.39
  95.5 0.2 copy.114
  95.7 0.7 copy.110
  (119 shorter events, 8.2 us)
Async XLA Ops:
  0.0 0.7 copy-start.2
  1.0 1.1 %copy-start.5 = (f32[128]{0:T(128)S(1)}, f32[128]{0:T(128)}, u32[]{:S(2)}) copy-start(f32[128]{0:T(128)} %param.13) | copy-start | bytes 1540
  1.0 1.1 %copy-start.6 = (s32[128]{0:T(128)S(1)}, s32[128]{0:T(128)}, u32[]{:S(2)}) copy-start(s32[128]{0:T(128)} %param.11) | copy-start | bytes 1540
  1.0 1.1 %copy-start.7 = (s32[128]{0:T(128)S(1)}, s32[128]{0:T(128)}, u32[]{:S(2)}) copy-start(s32[128]{0:T(128)} %param.12) | copy-start | bytes 1540
  1.0 1.4 %copy-start.1 = (s32[2,128,128]{2,1,0:T(8,128)S(1)}, s32[2,128,128]{2,1,0:T(8,128)}, u32[]{:S(2)}) copy-start(s32[2,128,128]{2,1,0:T(8,128)} %param.9) | copy-start | bytes 393220
  2.1 0.9 copy-start
  4.5 13.1 %all-to-all-start = ((f32[5,128,128]{2,0,1:T(8,128)}), f32[5,128,128]{2,0,1:T(8,128)S(1)}, u32[]{:S(2)}, u32[]{:S(2)}) async-start(f32[5,128,128]{2,0,1:T(8,128)} %pad_maximum_fusion), calls=%async_computation | async-start | bytes 1048576 | tf_op jit(solution)/shard_map/all_to_all | solution.py:96
  17.6 15.1 %all-to-all-start.3 = ((f32[3,128,128]{2,0,1:T(4,128)}), f32[3,128,128]{2,0,1:T(4,128)S(1)}, u32[]{:S(2)}, u32[]{:S(2)}) async-start(f32[3,128,128]{2,0,1:T(4,128)} %copy.98), calls=%async_computation.3 | async-start | bytes 524288 | tf_op jit(solution)/shard_map/all_to_all | solution.py:87
  24.5 0.7 copy-start.4
  32.7 7.9 %all-to-all-start.1 = ((f32[4,1,8192]{2,1,0:T(1,128)}), f32[4,1,8192]{2,1,0:T(1,128)S(1)}, u32[]{:S(2)}, u32[]{:S(2)}) async-start(f32[4,1,8192]{2,1,0:T(1,128)} %reshape.34), calls=%async_computation.1 | async-start | bytes 262144 | tf_op jit(solution)/shard_map/all_to_all | solution.py:100
  43.6 10.9 %all-to-all-start.2 = ((f32[2,128,128]{2,0,1:T(2,128)}), f32[2,128,128]{2,0,1:T(2,128)S(1)}, u32[]{:S(2)}, u32[]{:S(2)}) async-start(f32[2,128,128]{2,0,1:T(2,128)} %copy.94), calls=%async_computation.2 | async-start | bytes 262144 | tf_op jit(solution)/shard_map/all_to_all | solution.py:87
  54.6 0.7 copy-start.3
where the time goes:
time: 97 us; the launch traced here: 96.3 us
  waiting for transfers between devices  25.4 us (26%)
  blocking collectives  23.7 us (24%)
  local copies, waits for them, and re-layouts  18.9 us (19%)
  starting transfers between devices  17.6 us (18%)
  other arithmetic  9.41 us (10%)
  between operations  0.99 us (1%)
    all_to_all x2, waiting for transfers between devices, to_span(): lax.all_to_all(turned, 'span', split_axis=1, concat_axis=2, tiled=True)  13.2 us
    all_to_all x2, starting transfers between devices, to_span(): lax.all_to_all(turned, 'span', split_axis=1, concat_axis=2, tiled=True)  10 us
    all_to_all x1, blocking collectives, span_return(): lax.all_to_all(lines, 'span', split_axis=2, concat_axis=1, tiled=True)  9.74 us
    unnamed x26, local copies, waits for them, and re-layouts  9.18 us
    all_to_all x1, waiting for transfers between devices, to_chord(): lax.all_to_all(block, 'chord', split_axis=1, concat_axis=2, tiled=True)  7.84 us
    all_to_all x1, blocking collectives, to_chord(): lax.all_to_all(block, 'chord', split_axis=1, concat_axis=2, tiled=True)  6.99 us
    all_to_all x1, blocking collectives, from_chord(): lax.all_to_all(lines, 'chord', split_axis=2, concat_axis=1, tiled=True)  6.99 us
    all_to_all x1, waiting for transfers between devices, from_chord(): lax.all_to_all(lines, 'chord', split_axis=2, concat_axis=1, tiled=True)  4.36 us
  transfers between devices with their start and end apart: 4, of which 4 were waited for; matrix products, arithmetic and copies ran while one was open for 3% of the time, Pallas kernels for 0%

commit v1 on v0

--- a/solution.py
+++ b/solution.py
@@ -97,7 +97,12 @@
 
 
 def from_chord(lines):
-    return lax.all_to_all(lines, "chord", split_axis=2, concat_axis=1, tiled=True)
+    return jnp.concatenate(
+        lax.all_to_all(
+            jnp.stack(jnp.split(lines, lax.axis_size("chord"), 2), axis=0), "chord", 0, 0
+        ),
+        axis=1,
+    )
 
 
 def per_device(pressure, fill_state, perm_class, perm_table, inlet_span, inlet_chord, inlet_rate):

time: 97 us -> 92.7 us (0.956)
  local copies, waits for them, and re-layouts: 18.9 us -> 15.3 us
  other arithmetic: 9.41 us -> 8 us
    unnamed x26 -> x22, local copies, waits for them, and re-layouts: 9.18 us -> 6.53 us
    all_to_all x2 -> x0, other arithmetic: 2.04 us -> none  [from_chord(): lax.all_to_all(lines, 'chord', split_axis=2, concat_axis=1, tiled=True)]
    all_to_all x5 -> x0, local copies, waits for them, and re-layouts: 1.65 us -> none  [from_chord(): lax.all_to_all(lines, 'chord', split_axis=2, concat_axis=1, tiled=True)]
where the time goes in v1:
time: 92.7 us; the launch traced here: 92.1 us
  waiting for transfers between devices  26.2 us (28%)
  blocking collectives  23.7 us (26%)
  starting transfers between devices  17.6 us (19%)
  local copies, waits for them, and re-layouts  15.3 us (17%)
  other arithmetic  8 us (9%)
  between operations  0.96 us (1%)
    all_to_all x2, waiting for transfers between devices, to_span(): lax.all_to_all(turned, 'span', split_axis=1, concat_axis=2, tiled=True)  14 us
    all_to_all x2, starting transfers between devices, to_span(): lax.all_to_all(turned, 'span', split_axis=1, concat_axis=2, tiled=True)  10 us
    all_to_all x1, blocking collectives, span_return(): lax.all_to_all(lines, 'span', split_axis=2, concat_axis=1, tiled=True)  9.74 us
    all_to_all x1, waiting for transfers between devices, to_chord(): lax.all_to_all(block, 'chord', split_axis=1, concat_axis=2, tiled=True)  7.85 us
    all_to_all x1, blocking collectives, from_chord(): lax.all_to_all(jnp.stack(jnp.split(lines, lax.axis_size('chord'), 2), axi...  6.99 us
    all_to_all x1, blocking collectives, to_chord(): lax.all_to_all(block, 'chord', split_axis=1, concat_axis=2, tiled=True)  6.99 us
    unnamed x22, local copies, waits for them, and re-layouts  6.53 us
    all_to_all x1, waiting for transfers between devices, from_chord(): lax.all_to_all(jnp.stack(jnp.split(lines, lax.axis_size('chord'), 2), axi...  4.36 us
  transfers between devices with their start and end apart: 4, of which 4 were waited for; matrix products, arithmetic and copies ran while one was open for 3% of the time, Pallas kernels for 0%

profile of v1, /device:TPU:0, one launch (start us, length us, event | category | flops | bytes accessed | tf_op | source)
XLA Modules:
  0.0 92.1 jit_solution(2383944226805564542)
XLA Ops:
  0.0 0.7 copy-done.2
  0.7 0.3 slice_reduce_fusion.7
  1.0 1.0 %copy.104 = f32[2,128,128]{2,0,1:T(2,128)S(1)} copy(f32[2,128,128]{2,1,0:T(8,128)} %param.7) | data formatting | bytes 262144 | tf_op args[0]
  2.1 0.2 fusion.16
  2.4 0.6 copy-done
  3.0 0.6 fusion.13
  3.5 1.0 %pad_maximum_fusion = f32[5,128,128]{2,0,1:T(8,128)} fusion(f32[2,128,128]{2,0,1:T(2,128)S(1)} %copy.104, f32[1,128,128]{2,0,1:T(1,128)S(1)} %bitcast.128, f32[2,128,128]{2,0,1:T(2,128)S(1)} %fusion.13), kind=kLoop, calls=%fused_computation | loop fusion | flops 163840 | bytes 655360 | tf_op jit(solution)/shard_map/concatenate | solution.py:132
  4.5 4.3 %all-to-all-start = ((f32[5,128,128]{2,0,1:T(8,128)}), f32[5,128,128]{2,0,1:T(8,128)S(1)}, u32[]{:S(2)}, u32[]{:S(2)}) async-start(f32[5,128,128]{2,0,1:T(8,128)} %pad_maximum_fusion), calls=%async_computation | async-start | bytes 1048576 | tf_op jit(solution)/shard_map/all_to_all | solution.py:96
  8.9 0.8 copy.114
  9.8 7.8 %all-to-all-done = f32[5,128,128]{2,0,1:T(8,128)S(1)} async-done(((f32[5,128,128]{2,0,1:T(8,128)}), f32[5,128,128]{2,0,1:T(8,128)S(1)}, u32[]{:S(2)}, u32[]{:S(2)}) %all-to-all-start) | async-done | bytes 327712 | tf_op jit(solution)/shard_map/all_to_all | solution.py:96
  17.6 6.5 %all-to-all-start.3 = ((f32[3,128,128]{2,0,1:T(4,128)}), f32[3,128,128]{2,0,1:T(4,128)S(1)}, u32[]{:S(2)}, u32[]{:S(2)}) async-start(f32[3,128,128]{2,0,1:T(4,128)} %copy.114), calls=%async_computation.3 | async-start | bytes 524288 | tf_op jit(solution)/shard_map/all_to_all | solution.py:87
  24.5 0.6 copy-done.4
  25.2 0.1 fusion.2
  25.3 0.7 pad_maximum_fusion.1
  26.0 6.7 %all-to-all-done.3 = f32[3,128,128]{2,0,1:T(4,128)S(1)} async-done(((f32[3,128,128]{2,0,1:T(4,128)}), f32[3,128,128]{2,0,1:T(4,128)S(1)}, u32[]{:S(2)}, u32[]{:S(2)}) %all-to-all-start.3) | async-done | bytes 196640 | tf_op jit(solution)/shard_map/all_to_all | solution.py:87
  32.7 3.3 %all-to-all-start.1 = ((f32[4,2,32,128]{3,2,1,0:T(8,128)}), f32[4,2,32,128]{3,2,1,0:T(8,128)S(1)}, u32[]{:S(2)}, u32[]{:S(2)}) async-start(f32[4,2,32,128]{3,2,1,0:T(8,128)} %pad_maximum_fusion.1), calls=%async_computation.1 | async-start | bytes 262144 | tf_op jit(solution)/shard_map/all_to_all | solution.py:101
  36.2 4.4 %all-to-all-done.1 = f32[4,2,32,128]{3,2,1,0:T(8,128)S(1)} async-done(((f32[4,2,32,128]{3,2,1,0:T(8,128)}), f32[4,2,32,128]{3,2,1,0:T(8,128)S(1)}, u32[]{:S(2)}, u32[]{:S(2)}) %all-to-all-start.1) | async-done | bytes 131104 | tf_op jit(solution)/shard_map/all_to_all | solution.py:101
  40.6 0.8 copy.110
  41.4 3.6 %all-to-all-start.2 = ((f32[2,128,128]{2,0,1:T(2,128)}), f32[2,128,128]{2,0,1:T(2,128)S(1)}, u32[]{:S(2)}, u32[]{:S(2)}) async-start(f32[2,128,128]{2,0,1:T(2,128)} %copy.110), calls=%async_computation.2 | async-start | bytes 262144 | tf_op jit(solution)/shard_map/all_to_all | solution.py:87
  45.0 7.3 %all-to-all-done.2 = f32[2,128,128]{2,0,1:T(2,128)S(1)} async-done(((f32[2,128,128]{2,0,1:T(2,128)}), f32[2,128,128]{2,0,1:T(2,128)S(1)}, u32[]{:S(2)}, u32[]{:S(2)}) %all-to-all-start.2) | async-done | bytes 131104 | tf_op jit(solution)/shard_map/all_to_all | solution.py:87
  52.3 0.7 copy-done.3
  53.4 0.2 fusion.44
  53.6 0.1 fusion.60
  54.1 0.1 fusion.43
  54.6 0.1 fusion.42
  55.2 0.1 fusion.41
  55.8 0.1 fusion.40
  56.3 0.1 fusion.39
  56.9 0.1 fusion.38
  57.7 0.5 copy.118
  58.2 1.4 %reshape.50 = f32[8,1,4096]{2,1,0:T(1,128)S(1)} reshape(f32[1024,2,16]{2,1,0:T(2,128)S(1)} %bitcast.105) | data formatting | bytes 262144
  59.7 9.7 %all_to_all.94 = f32[8,1,4096]{2,1,0:T(1,128)S(1)} all-to-all(f32[8,1,4096]{2,1,0:T(1,128)S(1)} %reshape.50), channel_id=1, replica_groups=mesh['span'=8,'chord'=4] {'span'}, dimensions={0} | all-to-all | bytes 262144 | tf_op jit(solution)/shard_map/all_to_all | solution.py:91
  69.4 0.5 broadcast.342
  69.9 1.0 %reduce.16 = f32[8,4096]{1,0:T(8,128)S(1)} reduce(f32[8,1,4096]{2,1,0:T(1,128)S(1)} %all_to_all.94, f32[]{:T(128)} %broadcast.342), dimensions={1}, to_apply=%all_to_all.78.reduce_sub_computation | reduce | bytes 262148 | tf_op jit(solution)/shard_map/all_to_all | solution.py:91
  70.9 1.4 %reshape.51 = f32[1024,2,16]{2,1,0:T(2,128)S(1)} reshape(f32[8,4096]{1,0:T(8,128)S(1)} %reduce.16) | data formatting | bytes 262144
  72.3 0.4 copy.126
  72.8 7.0 %all_to_all.95 = f32[2,128,128]{2,0,1:T(2,128)S(1)} all-to-all(f32[2,128,128]{2,0,1:T(2,128)S(1)} %copy.121), channel_id=1, replica_groups=mesh['span'=8,'chord'=4] {'chord'}, dimensions={1} | all-to-all | bytes 262144 | tf_op jit(solution)/shard_map/all_to_all | solution.py:96
  79.8 0.1 negate_divide_fusion
  80.3 0.2 fusion.34
  80.5 0.1 fusion.74
  80.9 0.1 fusion.33
  81.5 0.1 fusion.32
  82.1 0.1 fusion.31
  82.6 0.1 fusion.30
  83.2 0.1 fusion.29
  83.8 0.1 fusion.28
  84.4 7.0 %all_to_all.96 = f32[4,2,32,128]{3,2,1,0:T(8,128)S(1)} all-to-all(f32[4,2,32,128]{3,2,1,0:T(8,128)S(1)} %pad_maximum_fusion.2), channel_id=1, replica_groups=mesh['span'=8,'chord'=4] {'chord'}, dimensions={0} | all-to-all | bytes 262144 | tf_op jit(solution)/shard_map/all_to_all | solution.py:101
  91.4 0.7 copy.124
  (113 shorter events, 7.0 us)
Async XLA Ops:
  0.0 0.7 copy-start.2
  1.0 1.1 %copy-start.5 = (f32[128]{0:T(128)S(1)}, f32[128]{0:T(128)}, u32[]{:S(2)}) copy-start(f32[128]{0:T(128)} %param.13) | copy-start | bytes 1540
  1.0 1.1 %copy-start.6 = (s32[128]{0:T(128)S(1)}, s32[128]{0:T(128)}, u32[]{:S(2)}) copy-start(s32[128]{0:T(128)} %param.11) | copy-start | bytes 1540
  1.0 1.1 %copy-start.7 = (s32[128]{0:T(128)S(1)}, s32[128]{0:T(128)}, u32[]{:S(2)}) copy-start(s32[128]{0:T(128)} %param.12) | copy-start | bytes 1540
  1.0 1.4 %copy-start.1 = (s32[2,128,128]{2,1,0:T(8,128)S(1)}, s32[2,128,128]{2,1,0:T(8,128)}, u32[]{:S(2)}) copy-start(s32[2,128,128]{2,1,0:T(8,128)} %param.9) | copy-start | bytes 393220
  2.1 0.9 copy-start
  4.5 13.1 %all-to-all-start = ((f32[5,128,128]{2,0,1:T(8,128)}), f32[5,128,128]{2,0,1:T(8,128)S(1)}, u32[]{:S(2)}, u32[]{:S(2)}) async-start(f32[5,128,128]{2,0,1:T(8,128)} %pad_maximum_fusion), calls=%async_computation | async-start | bytes 1048576 | tf_op jit(solution)/shard_map/all_to_all | solution.py:96
  17.6 15.1 %all-to-all-start.3 = ((f32[3,128,128]{2,0,1:T(4,128)}), f32[3,128,128]{2,0,1:T(4,128)S(1)}, u32[]{:S(2)}, u32[]{:S(2)}) async-start(f32[3,128,128]{2,0,1:T(4,128)} %copy.114), calls=%async_computation.3 | async-start | bytes 524288 | tf_op jit(solution)/shard_map/all_to_all | solution.py:87
  24.5 0.7 copy-start.4
  32.7 7.9 %all-to-all-start.1 = ((f32[4,2,32,128]{3,2,1,0:T(8,128)}), f32[4,2,32,128]{3,2,1,0:T(8,128)S(1)}, u32[]{:S(2)}, u32[]{:S(2)}) async-start(f32[4,2,32,128]{3,2,1,0:T(8,128)} %pad_maximum_fusion.1), calls=%async_computation.1 | async-start | bytes 262144 | tf_op jit(solution)/shard_map/all_to_all | solution.py:101
  41.4 10.9 %all-to-all-start.2 = ((f32[2,128,128]{2,0,1:T(2,128)}), f32[2,128,128]{2,0,1:T(2,128)S(1)}, u32[]{:S(2)}, u32[]{:S(2)}) async-start(f32[2,128,128]{2,0,1:T(2,128)} %copy.110), calls=%async_computation.2 | async-start | bytes 262144 | tf_op jit(solution)/shard_map/all_to_all | solution.py:87
  52.3 0.7 copy-start.3
